TPU v7x, 32 devices: a whole 2x2x4 slice. The times are simulated.
32 devices in a mesh: groups: 2 (over y), expert: 4 (over z), tensor: 4 (over x, core).
Axes of the slice: x: 2, y: 2, z: 4, core: 2. Of those that a mesh axis runs over, the one named last changes fastest.
Arguments:
- tokens: bfloat16 [1280, 3584], P(('groups', 'expert')), parts along dimension 0, may hold values from -6 to 6
- affinity: float32 [1280, 8], P(('groups', 'expert')), parts along dimension 0, may hold values from 0.05 to 1
- expert_ids: int32 [1280, 8], P(('groups', 'expert')), parts along dimension 0, may hold values from 0 to 255, as said below
- capacity: int32 [8], P('groups'), parts along dimension 0, may hold values from 4 to 8
- routed_gate: bfloat16 [4, 3584, 1024], P('expert', None, 'tensor'), may hold values from -0.09375 to 0.09375
- routed_up: bfloat16 [4, 3584, 1024], P('expert', None, 'tensor'), may hold values from -0.09375 to 0.09375
- routed_down: bfloat16 [4, 1024, 3584], P('expert', 'tensor'), may hold values from -0.1875 to 0.1875
- shared_gate: bfloat16 [3584, 2048], P('expert', 'tensor'), may hold values from -0.09375 to 0.09375
- shared_up: bfloat16 [3584, 2048], P('expert', 'tensor'), may hold values from -0.09375 to 0.09375
- shared_down_t: bfloat16 [3584, 2048], P('expert', 'tensor'), may hold values from -0.125 to 0.125
Outputs:
- mixed: bfloat16 [1280, 3584], P(('groups', 'expert'), 'tensor'), parts along dimension 0
There are 2 independent parts, one for each index of `groups`. A program takes and returns all parts, laid end to end along the dimension named above; an argument that names none is the same for every part. Nothing has to cross between parts.
Inputs may be any that keep to these rules, and one draw needn't show every extreme that they name: `expert_ids`: each row names 8 different experts.
All inputs are finite; a program needn't handle non-finite values.
Results may differ from a plain program's by a relative error of at most 0.014.
Values may be sent and summed in bfloat16 or wider, within the bound.
A program may use at most 64 MiB of HBM per device.

v0:
```python
import jax
import jax.numpy as jnp
from jax import lax
from jax.sharding import PartitionSpec as P

CAP = 8


def routing_tables(affinity, expert_ids, capacity):
    window = capacity.shape[0]
    tok_rows = expert_ids.shape[0]
    columns = jnp.arange(window, dtype=jnp.int32)
    matches = (expert_ids[:, :, None] == columns[None, None, :]).astype(jnp.float32)
    hit_mask = jnp.sum(matches, axis=1)
    route_weight = (
        2.5
        * jnp.sum(affinity[:, :, None] * matches, axis=1)
        / jnp.sum(affinity, axis=1, keepdims=True)
    )
    earlier = jnp.tril(jnp.ones((tok_rows, tok_rows), jnp.float32), -1)
    slot_index = jnp.dot(earlier, hit_mask, precision=lax.Precision.HIGHEST)
    kept_mask = hit_mask * (slot_index < capacity[None, :].astype(jnp.float32)).astype(jnp.float32)
    levels = jnp.arange(CAP, dtype=jnp.float32)
    placement = kept_mask.T[:, None, :] * (
        slot_index.T[:, None, :] == levels[None, :, None]
    ).astype(jnp.float32)
    return (placement, route_weight)


def local(
    tokens,
    affinity,
    expert_ids,
    capacity,
    routed_gate,
    routed_up,
    routed_down,
    shared_gate,
    shared_up,
    shared_down_t,
):
    gathered_gate, gathered_up, gathered_down = (
        lax.all_gather(shared_gate, "expert", axis=0, tiled=True),
        lax.all_gather(shared_up, "expert", axis=0, tiled=True),
        lax.all_gather(shared_down_t, "expert", axis=0, tiled=True),
    )
    placement, route_weight = routing_tables(affinity, expert_ids, capacity)
    placement_half = placement.astype(jnp.bfloat16)
    outgoing = jnp.einsum(
        "ect,td->ecd", placement_half, tokens, preferred_element_type=jnp.float32
    ).astype(jnp.bfloat16)
    received = lax.all_to_all(outgoing, "expert", split_axis=0, concat_axis=0, tiled=True)
    flat_rows = received.reshape(-1, received.shape[-1])
    gate_rows = jnp.dot(flat_rows, routed_gate[0], preferred_element_type=jnp.float32)
    up_rows = jnp.dot(flat_rows, routed_up[0], preferred_element_type=jnp.float32)
    activated = (jax.nn.silu(gate_rows) * up_rows).astype(jnp.bfloat16)
    partial_out = jnp.dot(activated, routed_down[0], preferred_element_type=jnp.float32)
    partial_out = partial_out.reshape(received.shape[0], received.shape[1], partial_out.shape[-1])
    owner_total = lax.psum_scatter(
        partial_out.astype(jnp.bfloat16), "tensor", scatter_dimension=2, tiled=True
    ).astype(jnp.float32)
    back_rows = lax.all_to_all(
        owner_total.astype(jnp.bfloat16), "expert", split_axis=0, concat_axis=0, tiled=True
    ).astype(owner_total.dtype)
    shared_gate_rows = jnp.dot(tokens, gathered_gate, preferred_element_type=jnp.float32)
    shared_up_rows = jnp.dot(tokens, gathered_up, preferred_element_type=jnp.float32)
    shared_hidden = (jax.nn.silu(shared_gate_rows) * shared_up_rows).astype(jnp.bfloat16)
    shared_out = lax.dot_general(
        shared_hidden, gathered_down, (((1,), (1,)), ((), ())), preferred_element_type=jnp.float32
    )
    weighted = placement * route_weight.T[:, None, :]
    routed_out = jnp.einsum("ect,ecd->td", weighted, back_rows, precision=lax.Precision.HIGHEST)
    summed = lax.psum_scatter(
        shared_out.astype(jnp.bfloat16), "tensor", scatter_dimension=1, tiled=True
    ).astype(jnp.float32)
    mixed_out = summed + routed_out
    return mixed_out.astype(jnp.bfloat16)


def solution(mesh):
    in_specs = (
        P(("groups", "expert"), None),
        P(("groups", "expert"), None),
        P(("groups", "expert"), None),
        P("groups"),
        P("expert", None, "tensor"),
        P("expert", None, "tensor"),
        P("expert", "tensor", None),
        P("expert", "tensor"),
        P("expert", "tensor"),
        P("expert", "tensor"),
    )
    out_specs = P(("groups", "expert"), "tensor")
    return jax.shard_map(local, mesh=mesh, in_specs=in_specs, out_specs=out_specs, check_vma=False)
```

profile of v0, /device:TPU:2, one launch (start us, length us, event | category | flops | bytes accessed | tf_op | source)
XLA Modules:
  0.0 273.6 jit_solution(10132125668353124512)
XLA Ops:
  7.4 0.0 copy-start
  7.4 0.0 copy-start.5
  7.4 0.0 copy-start.3
  7.4 0.0 copy-start.4
  7.4 0.0 copy-start.1
  7.4 0.0 all-gather.4.cloned.1.call-start
  7.4 0.7 all-gather.4.cloned.1.call-update
  8.1 0.0 all-gather.6.cloned.1.call-start
  8.2 0.7 all-gather.6.cloned.1.call-update
  8.9 0.0 all-gather.8.cloned.1.call-start
  8.9 0.7 all-gather.8.cloned.1.call-update
  9.6 0.0 reduce-scatter.9.cloned.1.call-start
  9.7 0.0 copy-done.5
  9.7 0.0 copy-start.2
  9.7 0.0 copy-done.3
  9.7 0.0 copy-done.4
  9.7 0.3 bitcast_select_fusion
  10.0 0.0 copy-done.1
  10.1 0.3 convolution_convert_fusion.2
  10.3 12.9 %all_to_all.10 = bf16[4,8,3584]{2,1,0:T(8,128)(2,1)S(1)} all-to-all(bf16[4,8,3584]{2,1,0:T(8,128)(2,1)S(1)} %convolution_convert_fusion.2), channel_id=1, replica_groups=mesh['groups'=2,'expert'=4,'tensor'=4] {'expert'}, dimensions={0} | all-to-all | bytes 458752 | tf_op jit(solution)/shard_map/all_to_all | solution.py:52
  23.3 0.0 copy-done.2
  23.3 0.4 fusion.3
  23.7 0.0 copy-done
  23.7 2.6 convolution_convert_fusion.1
  26.4 3.8 %copy.17 = bf16[4,8,3584]{1,0,2:T(4,128)(2,1)} copy(bf16[4,8,3584]{2,1,0:T(8,128)(2,1)S(1)} %convolution_convert_fusion.1) | data formatting | bytes 458752
  30.2 5.5 %reshape.19 = bf16[3584,32]{1,0:T(8,128)(2,1)} reshape(bf16[3584,4,8]{2,1,0:T(4,128)(2,1)} %bitcast.52) | data formatting | bytes 458752
  35.7 0.0 reduce-scatter.9.cloned.1.call-update
  35.8 0.0 reduce-scatter.7.cloned.1.call-start
  35.8 47.3 %all-gather.4.cloned.1.call-done = bf16[3584,512]{1,0:T(8,128)(2,1)} async-done(((bf16[896,512]{1,0:T(8,128)(2,1)}), bf16[3584,512]{1,0:T(8,128)(2,1)}) %all-gather.4.cloned.1.call-update) | async-done | bytes 3670032 | tf_op jit(solution)/shard_map/all_gather | solution.py:43
  83.1 2.8 %fusion.53 = f32[160,512]{1,0:T(8,128)S(1)} fusion(bf16[160,3584]{1,0:T(8,128)(2,1)S(1)} %copy-done.1, bf16[3584,512]{1,0:T(8,128)(2,1)} %all-gather.4.cloned.1.call-done), kind=kOutput, calls=%fused_computation.59 | convolution fusion | flops 587202560 | bytes 5144576 | tf_op jit(solution)/shard_map/dot_general | solution.py:65
  85.9 69.8 %all-gather.6.cloned.1.call-done = bf16[3584,512]{1,0:T(8,128)(2,1)} async-done(((bf16[896,512]{1,0:T(8,128)(2,1)}), bf16[3584,512]{1,0:T(8,128)(2,1)}) %all-gather.6.cloned.1.call-update) | async-done | bytes 3670032 | tf_op jit(solution)/shard_map/all_gather | solution.py:44
  155.7 72.3 %all-gather.8.cloned.1.call-done = bf16[3584,512]{1,0:T(8,128)(2,1)} async-done(((bf16[896,512]{1,0:T(8,128)(2,1)}), bf16[3584,512]{1,0:T(8,128)(2,1)}) %all-gather.8.cloned.1.call-update) | async-done | bytes 3670032 | tf_op jit(solution)/shard_map/all_gather | solution.py:45
  228.0 6.3 %convolution_convert_fusion = bf16[160,3584]{1,0:T(8,128)(2,1)} fusion(bf16[3584,512]{1,0:T(8,128)(2,1)} %all-gather.8.cloned.1.call-done, bf16[160,3584]{1,0:T(8,128)(2,1)S(1)} %copy-done.1, bf16[3584,512]{1,0:T(8,128)(2,1)} %all-gather.6.cloned.1.call-done, f32[160,512]{1,0:T(8,128)S(1)} %fusion.53), kind=kOutput, calls=%fused_computation | convolution fusion | flops 1175470080 | bytes 9961472 | tf_op jit(solution)/shard_map/dot_general | solution.py:68
  234.3 2.7 copy.15
  236.9 0.0 reduce-scatter.7.cloned.1.call-update
  237.0 0.0 reduce-scatter.9.cloned.1.call-done
  237.0 1.9 reshape.20
  239.0 1.5 copy.18
  240.5 3.3 %all-to-all-start.1 = ((bf16[4,8,896]{2,1,0:T(8,128)(2,1)}), bf16[4,8,896]{2,1,0:T(8,128)(2,1)S(1)}, u32[]{:S(2)}, u32[]{:S(2)}) async-start(bf16[4,8,896]{2,1,0:T(8,128)(2,1)} %copy.18), calls=%async_computation.1 | async-start | bytes 114688 | tf_op jit(solution)/shard_map/all_to_all | solution.py:62
  243.8 20.3 %reduce-scatter.7.cloned.1.call-done = bf16[896,160]{1,0:T(8,128)(2,1)} async-done(((bf16[3584,160]{1,0:T(8,128)(2,1)}), bf16[896,160]{1,0:T(8,128)(2,1)}) %reduce-scatter.7.cloned.1.call-update) | async-done | bytes 286736
  264.1 1.2 copy.16
  265.3 0.0 all-to-all-done.1
  265.3 1.2 fusion.6
  (5 shorter events, 0.1 us)
Async XLA Ops:
  7.4 16.4 %copy-start = (bf16[1,256,3584]{2,1,0:T(8,128)(2,1)S(1)}, bf16[1,256,3584]{2,1,0:T(8,128)(2,1)}, u32[]{:S(2)}) copy-start(bf16[1,256,3584]{2,1,0:T(8,128)(2,1)} %param.16) | copy-start | bytes 5505028
  7.4 2.3 copy-start.5
  7.4 2.3 copy-start.3
  7.4 2.3 copy-start.4
  7.4 2.7 copy-start.1
  7.4 75.7 %all-gather.4.cloned.1.call-start = ((), (), s32[]{:S(2)}) async-start(), calls=%async_computation.4 | async-start | bytes 4587520 | tf_op jit(solution)/shard_map/all_gather | solution.py:43
  8.1 147.6 %all-gather.6.cloned.1.call-start = ((), (), s32[]{:S(2)}) async-start(), calls=%async_computation.5 | async-start | bytes 4587520 | tf_op jit(solution)/shard_map/all_gather | solution.py:44
  8.9 219.1 %all-gather.8.cloned.1.call-start = ((), (), s32[]{:S(2)}) async-start(), calls=%async_computation.6 | async-start | bytes 4587520 | tf_op jit(solution)/shard_map/all_gather | solution.py:45
  9.6 227.4 %reduce-scatter.9.cloned.1.call-start = ((), (), s32[]{:S(2)}) async-start(), calls=%async_computation.8 | async-start | bytes 1146880
  9.7 13.6 %copy-start.2 = (bf16[1,3584,256]{2,1,0:T(8,128)(2,1)S(1)}, bf16[1,3584,256]{2,1,0:T(8,128)(2,1)}, u32[]{:S(2)}) copy-start(bf16[1,3584,256]{2,1,0:T(8,128)(2,1)} %param.14) | copy-start | bytes 5505028
  35.8 228.3 %reduce-scatter.7.cloned.1.call-start = ((), (), s32[]{:S(2)}) async-start(), calls=%async_computation.7 | async-start | bytes 2293760
  240.5 24.8 %all-to-all-start.1 = ((bf16[4,8,896]{2,1,0:T(8,128)(2,1)}), bf16[4,8,896]{2,1,0:T(8,128)(2,1)S(1)}, u32[]{:S(2)}, u32[]{:S(2)}) async-start(bf16[4,8,896]{2,1,0:T(8,128)(2,1)} %copy.18), calls=%async_computation.1 | async-start | bytes 114688 | tf_op jit(solution)/shard_map/all_to_all | solution.py:62
Sparse Core Ops, SparseCore 0:
  9.8 73.3 all-gather.3
  84.7 71.0 all-gather.5
  157.3 70.6 all-gather.7
Sparse Core Ops, SparseCore 1:
  35.8 25.2 reduce-scatter.8
  237.0 27.0 reduce-scatter.6
where the time goes:
time: 277 us; the launch traced here: 274 us
  waiting for transfers between devices  212 us (77%)
  local copies, waits for them, and re-layouts  16.8 us (6%)
  between operations  14.7 us (5%)
  matrix products  13.8 us (5%)
  blocking collectives  12.9 us (5%)
  starting transfers between devices  3.48 us (1%)
    all_gather x1, waiting for transfers between devices, local(): lax.all_gather(shared_down_t, 'expert', axis=0, tiled=True)  72.3 us
    all_gather x1, waiting for transfers between devices, local(): lax.all_gather(shared_up, 'expert', axis=0, tiled=True)  69.8 us
    all_gather x1, waiting for transfers between devices, local(): lax.all_gather(shared_gate, 'expert', axis=0, tiled=True)  47.3 us
    unnamed x7, waiting for transfers between devices  22.4 us
    unnamed x18, local copies, waits for them, and re-layouts  16.8 us
    all_to_all x1, blocking collectives, local(): lax.all_to_all(outgoing, 'expert', split_axis=0, concat_axis=0, tiled=True)  12.9 us
    dot_general x1, matrix products, local(): lax.dot_general(shared_hidden, gathered_down, (((1,), (1,)), ((), ())), p...  6.25 us
  transfers between devices with their start and end apart: 6, of which 4 were waited for; matrix products, arithmetic and copies ran while one was open for 11% of the time, Pallas kernels for 0%

commit v1 on v0

--- a/solution.py
+++ b/solution.py
@@ -39,10 +39,12 @@
     shared_up,
     shared_down_t,
 ):
-    gathered_gate, gathered_up, gathered_down = (
-        lax.all_gather(shared_gate, "expert", axis=0, tiled=True),
-        lax.all_gather(shared_up, "expert", axis=0, tiled=True),
-        lax.all_gather(shared_down_t, "expert", axis=0, tiled=True),
+    columns = lax.all_to_all(tokens, "expert", split_axis=1, concat_axis=0, tiled=True)
+    gate_part = jnp.dot(columns, shared_gate, preferred_element_type=jnp.float32)
+    up_part = jnp.dot(columns, shared_up, preferred_element_type=jnp.float32)
+    both_part = jnp.concatenate([gate_part, up_part], axis=1).astype(jnp.bfloat16)
+    both_rows = lax.psum_scatter(both_part, "expert", scatter_dimension=0, tiled=True).astype(
+        jnp.float32
     )
     placement, route_weight = routing_tables(affinity, expert_ids, capacity)
     placement_half = placement.astype(jnp.bfloat16)
@@ -62,12 +64,15 @@
     back_rows = lax.all_to_all(
         owner_total.astype(jnp.bfloat16), "expert", split_axis=0, concat_axis=0, tiled=True
     ).astype(owner_total.dtype)
-    shared_gate_rows = jnp.dot(tokens, gathered_gate, preferred_element_type=jnp.float32)
-    shared_up_rows = jnp.dot(tokens, gathered_up, preferred_element_type=jnp.float32)
-    shared_hidden = (jax.nn.silu(shared_gate_rows) * shared_up_rows).astype(jnp.bfloat16)
-    shared_out = lax.dot_general(
-        shared_hidden, gathered_down, (((1,), (1,)), ((), ())), preferred_element_type=jnp.float32
-    )
+    hidden_units = shared_gate.shape[1]
+    shared_hidden = (
+        jax.nn.silu(both_rows[:, :hidden_units]) * both_rows[:, hidden_units:]
+    ).astype(jnp.bfloat16)
+    hidden_all = lax.all_gather(shared_hidden, "expert", axis=0, tiled=True)
+    shared_cols = lax.dot_general(
+        hidden_all, shared_down_t, (((1,), (1,)), ((), ())), preferred_element_type=jnp.float32
+    ).astype(jnp.bfloat16)
+    shared_out = lax.all_to_all(shared_cols, "expert", split_axis=0, concat_axis=1, tiled=True)
     weighted = placement * route_weight.T[:, None, :]
     routed_out = jnp.einsum("ect,ecd->td", weighted, back_rows, precision=lax.Precision.HIGHEST)
     summed = lax.psum_scatter(

time: 277 us -> 186 us (0.67)
  waiting for transfers between devices: 212 us -> 74.7 us
  blocking collectives: 12.9 us -> 49.4 us
  starting transfers between devices: 3.48 us -> 11.8 us
  local copies, waits for them, and re-layouts: 16.8 us -> 19.8 us
  matrix products: 13.8 us -> 10.9 us
    all_gather x3 -> x0, waiting for transfers between devices: 189 us -> none  [the longest x1 72.3 us: local(): lax.all_gather(shared_down_t, 'expert', axis=0, tiled=True)]
    reduce_scatter x0 -> x1, waiting for transfers between devices: none -> 28.4 us  [local(): lax.psum_scatter(both_part, 'expert', scatter_dimension=0, tiled=True)]
    all_to_all x1, blocking collectives: 12.9 us -> 32.6 us  [local(): lax.all_to_all(tokens, 'expert', split_axis=1, concat_axis=0, tiled=True)]
    all_gather x0 -> x1, blocking collectives: none -> 16.7 us  [local(): hidden_all = lax.all_gather(shared_hidden, 'expert', axis=0, tiled=True)]
    unnamed x7 -> x5, waiting for transfers between devices: 22.4 us -> 35.2 us
    all_to_all x0 -> x2, waiting for transfers between devices: none -> 11.1 us  [the longest x1 11.1 us: local(): lax.all_to_all(shared_cols, 'expert', split_axis=0, concat_axis=1, tiled=...]
    all_to_all x0 -> x2, starting transfers between devices: none -> 6.91 us  [the longest x1 3.53 us: local(): lax.all_to_all(shared_cols, 'expert', split_axis=0, concat_axis=1, tiled=...]
    dot_general x2 -> x3, matrix products: 9.04 us -> 3.96 us  [the longest x1 1.89 us: local(): lax.dot_general(hidden_all, shared_down_t, (((1,), (1,)), ((), ())), pref...]
  transfers between devices with their start and end apart: 6 -> 6, of which waited for: 4 -> 4; matrix products, arithmetic and copies ran while one was open for 11% -> 13% of each run, Pallas kernels for 0% -> 0%
where the time goes in v1:
time: 186 us; the launch traced here: 183 us
  waiting for transfers between devices  74.7 us (40%)
  blocking collectives  49.4 us (27%)
  local copies, waits for them, and re-layouts  19.8 us (11%)
  between operations  15 us (8%)
  starting transfers between devices  11.8 us (6%)
  matrix products  10.9 us (6%)
    unnamed x5, waiting for transfers between devices  35.2 us
    all_to_all x1, blocking collectives, local(): lax.all_to_all(tokens, 'expert', split_axis=1, concat_axis=0, tiled=True)  32.6 us
    reduce_scatter x1, waiting for transfers between devices, local(): lax.psum_scatter(both_part, 'expert', scatter_dimension=0, tiled=True)  28.4 us
    unnamed x23, local copies, waits for them, and re-layouts  18.4 us
    all_gather x1, blocking collectives, local(): hidden_all = lax.all_gather(shared_hidden, 'expert', axis=0, tiled=True)  16.7 us
    all_to_all x1, waiting for transfers between devices, local(): lax.all_to_all(shared_cols, 'expert', split_axis=0, concat_axis=1, tiled=...  11.1 us
    all_to_all x1, starting transfers between devices, local(): lax.all_to_all(owner_total.astype(jnp.bfloat16), 'expert', split_axis=0,...  4.81 us
  transfers between devices with their start and end apart: 6, of which 4 were waited for; matrix products, arithmetic and copies ran while one was open for 13% of the time, Pallas kernels for 0%

profile of v1, /device:TPU:2, one launch (start us, length us, event | category | flops | bytes accessed | tf_op | source)
XLA Modules:
  0.0 182.9 jit_solution(15813552932231794479)
XLA Ops:
  7.4 0.0 copy-start
  7.4 0.0 reduce-scatter.10.cloned.1.call-start
  7.4 1.5 copy.42
  8.9 0.0 copy-start.4
  8.9 32.6 %all_to_all.48 = bf16[160,4,896]{2,0,1:T(8,128)(2,1)S(1)} all-to-all(bf16[160,4,896]{2,0,1:T(8,128)(2,1)S(1)} %bitcast.68), channel_id=1, replica_groups=mesh['groups'=2,'expert'=4,'tensor'=4] {'expert'}, dimensions={1} | all-to-all | bytes 2293760 | tf_op jit(solution)/shard_map/all_to_all | solution.py:42
  41.5 0.0 copy-done.4
  41.5 0.0 copy-start.5
  41.5 1.0 convolution_convert_fusion.3
  42.6 0.1 copy-done.5
  42.7 1.0 convolution_convert_fusion.4
  43.7 0.1 pad_maximum_fusion
  43.9 1.5 copy.32
  45.4 0.0 reduce-scatter.10.cloned.1.call-update
  45.4 0.6 copy-done.7
  46.1 0.1 copy-done.2
  46.1 0.0 copy-done.3
  46.2 0.3 bitcast_select_fusion
  46.4 0.3 copy-done.1
  46.7 1.0 convolution_convert_fusion.1
  47.7 3.4 %all-to-all-start.2 = ((bf16[4,8,3584]{2,1,0:T(8,128)(2,1)}), bf16[4,8,3584]{2,1,0:T(8,128)(2,1)S(1)}, u32[]{:S(2)}, u32[]{:S(2)}) async-start(bf16[4,8,3584]{2,1,0:T(8,128)(2,1)} %convolution_convert_fusion.1), calls=%async_computation.2 | async-start | bytes 458752 | tf_op jit(solution)/shard_map/all_to_all | solution.py:54
  51.1 0.0 copy-start.6
  51.1 28.4 %reduce-scatter.10.cloned.1.call-done = bf16[160,1024]{1,0:T(8,128)(2,1)} async-done(((bf16[640,1024]{1,0:T(8,128)(2,1)}), bf16[160,1024]{1,0:T(8,128)(2,1)}) %reduce-scatter.10.cloned.1.call-update) | async-done | bytes 327696 | tf_op jit(solution)/shard_map/reduce_scatter | solution.py:46
  79.5 1.0 convert_element_type.40
  80.5 0.1 fusion.19
  80.6 16.7 %all_gather.3 = bf16[640,512]{1,0:T(8,128)(2,1)S(1)} all-gather(bf16[160,512]{1,0:T(8,128)(2,1)S(1)} %fusion.19), channel_id=1, replica_groups=mesh['groups'=2,'expert'=4,'tensor'=4] {'expert'}, dimensions={0}, use_global_device_ids=true | all-gather | bytes 819200 | tf_op jit(solution)/shard_map/all_gather | solution.py:71
  97.4 0.0 copy-done.6
  97.4 1.9 %convolution_convert_fusion.2 = bf16[640,896]{1,0:T(8,128)(2,1)} fusion(bf16[640,512]{1,0:T(8,128)(2,1)S(1)} %all_gather.3, bf16[896,512]{1,0:T(8,128)(2,1)S(1)} %copy-done.6), kind=kOutput, calls=%fused_computation.7 | convolution fusion | flops 587776000 | bytes 2719744 | tf_op jit(solution)/shard_map/dot_general | solution.py:72
  99.3 0.0 all-to-all-done.2
  99.3 3.5 %all-to-all-start.1 = ((bf16[4,160,896]{2,1,0:T(8,128)(2,1)}), bf16[4,160,896]{2,1,0:T(8,128)(2,1)S(1)}, u32[]{:S(2)}, u32[]{:S(2)}) async-start(bf16[4,160,896]{2,1,0:T(8,128)(2,1)} %bitcast.71), calls=%async_computation.1 | async-start | bytes 2293760 | tf_op jit(solution)/shard_map/all_to_all | solution.py:75
  102.8 0.0 reduce-scatter.14.cloned.1.call-start
  102.9 1.9 %fusion.3 = f32[32,256]{1,0:T(8,128)S(1)} fusion(bf16[1,3584,256]{2,1,0:T(8,128)(2,1)} %param.14, bf16[4,8,3584]{2,1,0:T(8,128)(2,1)S(1)} %all-to-all-done.2), kind=kOutput, calls=%fused_computation.5 | convolution fusion | flops 58720256 | bytes 2097152 | tf_op jit(solution)/shard_map/dot_general | solution.py:56
  104.8 0.0 copy-done
  104.8 2.6 %convolution_convert_fusion = bf16[4,8,3584]{2,1,0:T(8,128)(2,1)S(1)} fusion(bf16[1,256,3584]{2,1,0:T(8,128)(2,1)S(1)} %copy-done, bf16[1,3584,256]{2,1,0:T(8,128)(2,1)} %param.15, bf16[4,8,3584]{2,1,0:T(8,128)(2,1)S(1)} %all-to-all-done.2, f32[32,256]{1,0:T(8,128)S(1)} %fusion.3), kind=kOutput, calls=%fused_computation | convolution fusion | flops 117604352 | bytes 4161536 | tf_op jit(solution)/shard_map/dot_general | solution.py:59
  107.4 3.8 %copy.36 = bf16[4,8,3584]{1,0,2:T(4,128)(2,1)} copy(bf16[4,8,3584]{2,1,0:T(8,128)(2,1)S(1)} %convolution_convert_fusion) | data formatting | bytes 458752
  111.2 5.5 %reshape.27 = bf16[3584,32]{1,0:T(8,128)(2,1)} reshape(bf16[3584,4,8]{2,1,0:T(4,128)(2,1)} %bitcast.65) | data formatting | bytes 458752
  116.7 0.0 reduce-scatter.14.cloned.1.call-update
  116.7 0.0 reduce-scatter.12.cloned.1.call-start
  116.8 11.1 %all-to-all-done.1 = bf16[4,160,896]{2,1,0:T(8,128)(2,1)S(1)} async-done(((bf16[4,160,896]{2,1,0:T(8,128)(2,1)}), bf16[4,160,896]{2,1,0:T(8,128)(2,1)S(1)}, u32[]{:S(2)}, u32[]{:S(2)}) %all-to-all-start.1) | async-done | bytes 1146912 | tf_op jit(solution)/shard_map/all_to_all | solution.py:75
  127.9 1.7 copy.38
  129.6 0.0 reduce-scatter.12.cloned.1.call-update
  129.6 11.4 %reduce-scatter.14.cloned.1.call-done = bf16[896,32]{1,0:T(8,128)(2,1)} async-done(((bf16[3584,32]{1,0:T(8,128)(2,1)}), bf16[896,32]{1,0:T(8,128)(2,1)}) %reduce-scatter.14.cloned.1.call-update) | async-done | bytes 57360
  141.0 1.9 %reshape.28 = bf16[896,4,8]{2,1,0:T(4,128)(2,1)S(1)} reshape(bf16[896,32]{1,0:T(8,128)(2,1)} %reduce-scatter.14.cloned.1.call-done) | data formatting | bytes 114688
  143.0 1.5 copy.37
  144.5 4.8 %all-to-all-start.3 = ((bf16[4,8,896]{2,1,0:T(8,128)(2,1)}), bf16[4,8,896]{2,1,0:T(8,128)(2,1)S(1)}, u32[]{:S(2)}, u32[]{:S(2)}) async-start(bf16[4,8,896]{2,1,0:T(8,128)(2,1)} %copy.37), calls=%async_computation.3 | async-start | bytes 114688 | tf_op jit(solution)/shard_map/all_to_all | solution.py:64
  149.3 23.7 %reduce-scatter.12.cloned.1.call-done = bf16[896,160]{1,0:T(8,128)(2,1)} async-done(((bf16[3584,160]{1,0:T(8,128)(2,1)}), bf16[896,160]{1,0:T(8,128)(2,1)}) %reduce-scatter.12.cloned.1.call-update) | async-done | bytes 286736
  173.1 1.2 copy.35
  174.3 0.0 all-to-all-done.3
  174.3 1.2 fusion.6
  (9 shorter events, 0.1 us)
Async XLA Ops:
  7.4 97.4 %copy-start = (bf16[1,256,3584]{2,1,0:T(8,128)(2,1)S(1)}, bf16[1,256,3584]{2,1,0:T(8,128)(2,1)}, u32[]{:S(2)}) copy-start(bf16[1,256,3584]{2,1,0:T(8,128)(2,1)} %param.16) | copy-start | bytes 5505028
  7.4 72.1 %reduce-scatter.10.cloned.1.call-start = ((), (), s32[]{:S(2)}) async-start(), calls=%async_computation.7 | async-start | bytes 1638400 | tf_op jit(solution)/shard_map/reduce_scatter | solution.py:46
  8.9 32.6 %copy-start.4 = (bf16[896,512]{1,0:T(8,128)(2,1)S(1)}, bf16[896,512]{1,0:T(8,128)(2,1)}, u32[]{:S(2)}) copy-start(bf16[896,512]{1,0:T(8,128)(2,1)} %param.18) | copy-start | bytes 2752516
  41.5 1.2 copy-start.5
  45.4 0.7 copy-start.7
  45.4 0.7 copy-start.2
  45.4 0.7 copy-start.3
  45.4 1.3 copy-start.1
  47.7 51.6 %all-to-all-start.2 = ((bf16[4,8,3584]{2,1,0:T(8,128)(2,1)}), bf16[4,8,3584]{2,1,0:T(8,128)(2,1)S(1)}, u32[]{:S(2)}, u32[]{:S(2)}) async-start(bf16[4,8,3584]{2,1,0:T(8,128)(2,1)} %convolution_convert_fusion.1), calls=%async_computation.2 | async-start | bytes 458752 | tf_op jit(solution)/shard_map/all_to_all | solution.py:54
  51.1 46.3 %copy-start.6 = (bf16[896,512]{1,0:T(8,128)(2,1)S(1)}, bf16[896,512]{1,0:T(8,128)(2,1)}, u32[]{:S(2)}) copy-start(bf16[896,512]{1,0:T(8,128)(2,1)} %param.19) | copy-start | bytes 2752516
  99.3 28.6 %all-to-all-start.1 = ((bf16[4,160,896]{2,1,0:T(8,128)(2,1)}), bf16[4,160,896]{2,1,0:T(8,128)(2,1)S(1)}, u32[]{:S(2)}, u32[]{:S(2)}) async-start(bf16[4,160,896]{2,1,0:T(8,128)(2,1)} %bitcast.71), calls=%async_computation.1 | async-start | bytes 2293760 | tf_op jit(solution)/shard_map/all_to_all | solution.py:75
  102.8 38.2 %reduce-scatter.14.cloned.1.call-start = ((), (), s32[]{:S(2)}) async-start(), calls=%async_computation.9 | async-start | bytes 1146880
  116.7 56.3 %reduce-scatter.12.cloned.1.call-start = ((), (), s32[]{:S(2)}) async-start(), calls=%async_computation.8 | async-start | bytes 2293760
  144.5 29.7 %all-to-all-start.3 = ((bf16[4,8,896]{2,1,0:T(8,128)(2,1)}), bf16[4,8,896]{2,1,0:T(8,128)(2,1)S(1)}, u32[]{:S(2)}, u32[]{:S(2)}) async-start(bf16[4,8,896]{2,1,0:T(8,128)(2,1)} %copy.37), calls=%async_computation.3 | async-start | bytes 114688 | tf_op jit(solution)/shard_map/all_to_all | solution.py:64
Sparse Core Ops, SparseCore 0:
  45.6 33.8 reduce-scatter.9
Sparse Core Ops, SparseCore 1:
  116.8 24.1 reduce-scatter.13
  143.4 29.6 reduce-scatter.11

commit v2 on v0

--- a/solution.py
+++ b/solution.py
@@ -1,6 +1,10 @@
+import functools
+
 import jax
 import jax.numpy as jnp
 from jax import lax
+from jax.experimental import pallas as pl
+from jax.experimental.pallas import tpu as pltpu
 from jax.sharding import PartitionSpec as P
 
 CAP = 8
@@ -77,6 +81,339 @@
     return mixed_out.astype(jnp.bfloat16)
 
 
+MESH = pl.DeviceIdType.MESH
+F32 = jnp.float32
+BF16 = jnp.bfloat16
+
+
+def remote(src, dst, send_sem, recv_sem, **device):
+    return pltpu.make_async_remote_copy(
+        src_ref=src,
+        dst_ref=dst,
+        send_sem=send_sem,
+        recv_sem=recv_sem,
+        device_id=device,
+        device_id_type=MESH,
+    )
+
+
+def fused_kernel(
+    n_exp, n_ten,
+    tok_any, aff_ref, ids_ref, cap_ref, rg_any, ru_any, rd_any, sg_any, su_any, sd_any,
+    out_ref,
+    tok, wgu, wdn, rgw, ruw, rdw, xall, gown, gsend, gin, hall, weights,
+    rout, rin, ys, yin, yb, back, acc, osend, oin, rsend, rfin, routed,
+    lsem, ax_s, ax_r, af_s, af_r, bx_s, bx_r, bf_s, bf_r, c_s, c_r, h_s, h_r,
+    y_s, y_r, k_s, k_r, o_s, o_r, t_s, t_r,
+):
+    e, t = lax.axis_index("expert"), lax.axis_index("tensor")
+    core = lax.rem(t, 2)
+    partner = t + 1 - 2 * core
+    rows, width = tok.shape
+    cols = width // n_exp
+    half = rows // 2
+    half_width = width // 2
+    hidden = hall.shape[2]
+    others = range(1, n_exp)
+
+    def up(k):
+        return lax.rem(e + k, n_exp)
+
+    def down(k):
+        return lax.rem(e - k + n_exp, n_exp)
+
+    def span(index, size, unit=128):
+        return pl.ds(pl.multiple_of(index * size, unit), size)
+
+    loads = [
+        pltpu.make_async_copy(tok_any, tok, lsem.at[0]),
+        pltpu.make_async_copy(sg_any, wgu.at[:, pl.ds(0, hidden)], lsem.at[1]),
+        pltpu.make_async_copy(su_any, wgu.at[:, pl.ds(hidden, hidden)], lsem.at[2]),
+        pltpu.make_async_copy(rg_any.at[0], rgw, lsem.at[3]),
+        pltpu.make_async_copy(ru_any.at[0], ruw, lsem.at[4]),
+        pltpu.make_async_copy(rd_any.at[0], rdw, lsem.at[5]),
+        pltpu.make_async_copy(sd_any, wdn, lsem.at[6]),
+    ]
+    for load in loads:
+        load.start()
+
+    barrier = pltpu.get_barrier_semaphore()
+    for k in others:
+        pl.semaphore_signal(barrier, inc=1, device_id={"expert": up(k)}, device_id_type=MESH)
+    for k in range(1, n_ten):
+        pl.semaphore_signal(
+            barrier, inc=1, device_id={"tensor": lax.rem(t + k, n_ten)}, device_id_type=MESH
+        )
+
+    @pl.when(e != t)
+    def _():
+        pl.semaphore_signal(
+            barrier, inc=1, device_id={"expert": t, "tensor": e}, device_id_type=MESH
+        )
+
+    pl.semaphore_wait(barrier, n_exp + n_ten - 2 + (e != t).astype(jnp.int32))
+
+    mine = span(core, half, 16)
+    a_copy = {}
+    for k in others:
+        a_copy[k] = remote(
+            tok_any.at[mine, span(up(k), cols)], xall.at[e, mine, :],
+            ax_s.at[k - 1], ax_r.at[k - 1], expert=up(k),
+        )
+        a_copy[k].start()
+
+    lanes = n_exp * CAP
+    column = lax.broadcasted_iota(jnp.int32, (rows, lanes), 1)
+    expert_of, level = column // CAP, lax.rem(column, CAP)
+    ids, aff = ids_ref[...], aff_ref[...]
+    hit = jnp.zeros((rows, lanes), F32)
+    chosen = jnp.zeros((rows, lanes), F32)
+    for k in range(ids.shape[1]):
+        match = (ids[:, k : k + 1] == expert_of).astype(F32)
+        hit += match
+        chosen += match * aff[:, k : k + 1]
+    share = 2.5 * chosen / jnp.sum(aff, axis=1, keepdims=True)
+    earlier = (
+        lax.broadcasted_iota(jnp.int32, (rows, rows), 1)
+        < lax.broadcasted_iota(jnp.int32, (rows, rows), 0)
+    ).astype(BF16)
+    slot = jnp.dot(earlier, hit.astype(BF16), preferred_element_type=F32)
+    limit = jnp.zeros((rows, lanes), jnp.int32)
+    for k in range(n_exp):
+        limit = jnp.where(expert_of == k, cap_ref[k], limit)
+    placed = (
+        hit * (slot < limit.astype(F32)).astype(F32) * (slot == level.astype(F32)).astype(F32)
+    )
+    weights[...] = placed * share
+    loads[0].wait()
+    chosen_rows = jnp.dot(
+        jnp.transpose(placed).astype(BF16), tok[...], preferred_element_type=F32
+    ).astype(BF16).astype(F32)
+    for k in range(n_exp):
+        rout[k] = chosen_rows[k * CAP : (k + 1) * CAP].astype(BF16)
+    side = span(core, half_width)
+    b_copy = {}
+    for k in others:
+        b_copy[k] = remote(
+            rout.at[up(k), :, side], rin.at[e, :, side],
+            bx_s.at[k - 1], bx_r.at[k - 1], expert=up(k),
+        )
+        b_copy[k].start()
+    rin[e] = rout[e]
+
+    order = [k for k in others if k != n_exp // 2] + [n_exp // 2]
+    af_copy, bf_copy = {}, {}
+    for k in order:
+        a_copy[k].wait_recv()
+        af_copy[k] = remote(
+            xall.at[down(k), mine, :], xall.at[down(k), mine, :],
+            af_s.at[k - 1], af_r.at[k - 1], tensor=partner,
+        )
+        af_copy[k].start()
+    loads[1].wait()
+    loads[2].wait()
+    c_copy = {}
+    for k in order:
+        af_copy[k].wait_recv()
+        gsend[k - 1] = jnp.dot(
+            xall[down(k)], wgu[...], preferred_element_type=F32
+        ).astype(BF16)
+        c_copy[k] = remote(
+            gsend.at[k - 1], gin.at[k - 1], c_s.at[k - 1], c_r.at[k - 1], expert=down(k)
+        )
+        c_copy[k].start()
+    for k in order:
+        b_copy[k].wait_recv()
+        bf_copy[k] = remote(
+            rin.at[down(k), :, side], rin.at[down(k), :, side],
+            bf_s.at[k - 1], bf_r.at[k - 1], tensor=partner,
+        )
+        bf_copy[k].start()
+    gown[...] = jnp.dot(tok[:, span(e, cols)], wgu[...], preferred_element_type=F32)
+
+    for load in loads[3:]:
+        load.wait()
+    for k in order:
+        bf_copy[k].wait_recv()
+    flat = jnp.concatenate([rin[k].astype(F32) for k in range(n_exp)], axis=0).astype(BF16)
+    gate = jnp.dot(flat, rgw[...], preferred_element_type=F32)
+    upper = jnp.dot(flat, ruw[...], preferred_element_type=F32)
+    act = (gate * (1.0 / (1.0 + jnp.exp(-gate))) * upper).astype(BF16)
+    ys[...] = jnp.dot(act, rdw[...], preferred_element_type=F32).astype(BF16)
+    y_copy = {}
+    part = width // n_ten
+    for k in range(1, n_ten):
+        to = lax.rem(t + k, n_ten)
+        y_copy[k] = remote(
+            ys.at[:, span(to, part)], yin.at[k - 1], y_s.at[k - 1], y_r.at[k - 1], tensor=to
+        )
+        y_copy[k].start()
+
+    both = gown[...]
+    for k in order:
+        c_copy[k].wait_recv()
+        both = both + gin[k - 1].astype(F32)
+    gate = both[:, :hidden]
+    hall[e] = (gate * (1.0 / (1.0 + jnp.exp(-gate))) * both[:, hidden:]).astype(BF16)
+    h_copy = {}
+    for k in others:
+        h_copy[k] = remote(
+            hall.at[e], hall.at[e], h_s.at[k - 1], h_r.at[k - 1], expert=up(k)
+        )
+        h_copy[k].start()
+
+    total = ys[:, span(t, part)].astype(F32)
+    for k in range(1, n_ten):
+        y_copy[k].wait_recv()
+        total = total + yin[k - 1].astype(F32)
+    for k in range(n_exp):
+        yb[k] = total[k * CAP : (k + 1) * CAP].astype(BF16)
+    k_copy = {}
+    for k in others:
+        k_copy[k] = remote(
+            yb.at[up(k)], back.at[e], k_s.at[k - 1], k_r.at[k - 1], expert=up(k)
+        )
+        k_copy[k].start()
+    back[e] = yb[e]
+
+    for k in order:
+        h_copy[k].wait_recv()
+
+    def product(index):
+        return lax.dot_general(
+            hall[index], wdn[...], (((1,), (1,)), ((), ())), preferred_element_type=F32
+        )
+
+    o_copy = []
+    bits = n_ten.bit_length() - 1
+    place = 0
+    for s in range(bits):
+        bit = lax.rem(t // (1 << s), 2)
+        low = lax.rem(t, 1 << s)
+        peer = t + (1 - 2 * bit) * (1 << s)
+        count = n_ten >> (s + 1)
+        copies = []
+        for i in range(count):
+            sent = (2 * i + 1 - bit) * (1 << s) + low
+            osend[place + i] = (product(sent) if s == 0 else acc[sent]).astype(BF16)
+            copy = remote(
+                osend.at[place + i], oin.at[place + i],
+                o_s.at[place + i], o_r.at[place + i], tensor=peer,
+            )
+            copy.start()
+            copies.append(copy)
+        if s == 0:
+            for i in range(count):
+                kept = 2 * i + bit
+                acc[kept] = product(kept)
+        for i in range(count):
+            kept = (2 * i + bit) * (1 << s) + low
+            copies[i].wait_recv()
+            acc[kept] = acc[kept] + oin[place + i].astype(F32)
+        o_copy += copies
+        place += count
+    final = remote(rsend, rfin, t_s, t_r, expert=t, tensor=e)
+
+    @pl.when(e != t)
+    def _():
+        rsend[...] = acc[t].astype(BF16)
+        final.start()
+
+    @pl.when(e == t)
+    def _():
+        rfin[...] = acc[t].astype(BF16)
+
+    for k in order:
+        k_copy[k].wait_recv()
+    rows_back = jnp.concatenate([back[k].astype(F32) for k in range(n_exp)], axis=0)
+    routed[...] = jnp.dot(
+        weights[...], rows_back, preferred_element_type=F32, precision=lax.Precision.HIGHEST
+    )
+
+    @pl.when(e != t)
+    def _():
+        final.wait()
+
+    out_ref[...] = (rfin[...].astype(F32) + routed[...]).astype(BF16)
+    for group in (a_copy, af_copy, b_copy, bf_copy, c_copy, h_copy, y_copy, k_copy):
+        for copy in group.values():
+            copy.wait_send()
+    for copy in o_copy:
+        copy.wait_send()
+
+
+def fused(n_exp, n_ten, *args):
+    tokens, affinity, expert_ids, capacity, rg, ru, rd, sg, su, sd = args
+    rows, width = tokens.shape
+    hidden = sg.shape[1]
+    cols, part = width // n_exp, width // n_ten
+    any_spec = pl.BlockSpec(memory_space=pl.ANY)
+    vmem = pl.BlockSpec(memory_space=pltpu.VMEM)
+    scratch = [
+        pltpu.VMEM((rows, width), BF16),
+        pltpu.VMEM((cols, 2 * hidden), BF16),
+        pltpu.VMEM((cols, hidden), BF16),
+        pltpu.VMEM(rg.shape[1:], BF16),
+        pltpu.VMEM(ru.shape[1:], BF16),
+        pltpu.VMEM(rd.shape[1:], BF16),
+        pltpu.VMEM((n_exp, rows, cols), BF16),
+        pltpu.VMEM((rows, 2 * hidden), F32),
+        pltpu.VMEM((n_exp - 1, rows, 2 * hidden), BF16),
+        pltpu.VMEM((n_exp - 1, rows, 2 * hidden), BF16),
+        pltpu.VMEM((n_exp, rows, hidden), BF16),
+        pltpu.VMEM((rows, n_exp * CAP), F32),
+        pltpu.VMEM((n_exp, CAP, width), BF16),
+        pltpu.VMEM((n_exp, CAP, width), BF16),
+        pltpu.VMEM((n_exp * CAP, width), BF16),
+        pltpu.VMEM((n_ten - 1, n_exp * CAP, part), BF16),
+        pltpu.VMEM((n_exp, CAP, part), BF16),
+        pltpu.VMEM((n_exp, CAP, part), BF16),
+        pltpu.VMEM((n_ten, rows, part), F32),
+        pltpu.VMEM((n_ten - 1, rows, part), BF16),
+        pltpu.VMEM((n_ten - 1, rows, part), BF16),
+        pltpu.VMEM((rows, part), BF16),
+        pltpu.VMEM((rows, part), BF16),
+        pltpu.VMEM((rows, part), F32),
+        pltpu.SemaphoreType.DMA((7,)),
+    ]
+    scratch += [pltpu.SemaphoreType.DMA((n_exp - 1,))] * 12
+    scratch += [pltpu.SemaphoreType.DMA((n_ten - 1,))] * 2
+    scratch += [pltpu.SemaphoreType.DMA((n_exp - 1,))] * 2
+    scratch += [pltpu.SemaphoreType.DMA((n_ten - 1,))] * 2
+    scratch += [pltpu.SemaphoreType.DMA] * 2
+    return pl.pallas_call(
+        functools.partial(fused_kernel, n_exp, n_ten),
+        out_shape=jax.ShapeDtypeStruct((rows, part), BF16),
+        in_specs=[any_spec, vmem, vmem, pl.BlockSpec(memory_space=pltpu.SMEM)] + [any_spec] * 6,
+        out_specs=vmem,
+        scratch_shapes=scratch,
+        compiler_params=pltpu.CompilerParams(
+            collective_id=0, has_side_effects=True, vmem_limit_bytes=48 * 1024 * 1024
+        ),
+    )(*args)
+
+
+def fits(n_exp, n_ten, tokens, capacity, routed_gate, shared_gate):
+    rows, width = tokens.shape
+    return (
+        n_exp == n_ten
+        and n_ten >= 2
+        and n_ten & (n_ten - 1) == 0
+        and capacity.shape[0] == n_exp
+        and routed_gate.shape[0] == 1
+        and rows % 32 == 0
+        and width % 256 == 0
+        and width % (128 * n_exp) == 0
+        and shared_gate.shape[1] % 128 == 0
+    )
+
+
+def layer(n_exp, n_ten, *args):
+    if fits(n_exp, n_ten, args[0], args[3], args[4], args[7]):
+        return fused(n_exp, n_ten, *args)
+    return local(*args)
+
+
 def solution(mesh):
     in_specs = (
         P(("groups", "expert"), None),
@@ -91,4 +428,5 @@
         P("expert", "tensor"),
     )
     out_specs = P(("groups", "expert"), "tensor")
-    return jax.shard_map(local, mesh=mesh, in_specs=in_specs, out_specs=out_specs, check_vma=False)
+    body = functools.partial(layer, mesh.shape["expert"], mesh.shape["tensor"])
+    return jax.shard_map(body, mesh=mesh, in_specs=in_specs, out_specs=out_specs, check_vma=False)

time: 277 us -> 97.4 us (0.35); the launches traced: 274 us -> 97 us
  waiting for transfers between devices: 212 us -> 0 us
  Pallas kernels: 0 us -> 87.7 us
  between operations: 14.7 us -> 0.04 us
  matrix products: 13.8 us -> 0 us
  blocking collectives: 12.9 us -> 0 us
  local copies, waits for them, and re-layouts: 16.8 us -> 9.25 us
  starting transfers between devices: 3.48 us -> 0 us
    all_gather x3 -> x0, waiting for transfers between devices: 189 us -> none  [the longest x1 72.3 us: local(): lax.all_gather(shared_down_t, 'expert', axis=0, tiled=True)]
    pallas_call x0 -> x1, Pallas kernels: none -> 87.7 us  [fused(): pl.pallas_call(functools.partial(fused_kernel, n_exp, n_ten), out_shape=j...]
    unnamed x7 -> x0, waiting for transfers between devices: 22.4 us -> none
    dot_general x7 -> x0, matrix products: 13.8 us -> none  [the longest x1 6.25 us: local(): lax.dot_general(shared_hidden, gathered_down, (((1,), (1,)), ((), ())), p...]
    all_to_all x1 -> x0, blocking collectives: 12.9 us -> none  [local(): lax.all_to_all(outgoing, 'expert', split_axis=0, concat_axis=0, tiled=True)]
    unnamed x18 -> x15, local copies, waits for them, and re-layouts: 16.8 us -> 9.25 us
    all_to_all x1 -> x0, starting transfers between devices: 3.28 us -> none  [local(): lax.all_to_all(owner_total.astype(jnp.bfloat16), 'expert', split_axis=0,...]
  transfers between devices with their start and end apart: 6 -> 0, of which waited for: 4 -> 0; matrix products, arithmetic and copies ran while one was open for 11% -> 0% of each run, Pallas kernels for 0% -> 0%
where the time goes in v2:
time: 97.4 us; the launch traced here: 97 us
  Pallas kernels  87.7 us (90%)
  local copies, waits for them, and re-layouts  9.25 us (9%)
    pallas_call x1, Pallas kernels, fused(): pl.pallas_call(functools.partial(fused_kernel, n_exp, n_ten), out_shape=j...  87.7 us
    unnamed x15, local copies, waits for them, and re-layouts  9.25 us

profile of v2, /device:TPU:2, one launch (start us, length us, event | category | flops | bytes accessed | tf_op | source)
XLA Modules:
  0.0 97.0 jit_solution(13242000168729862069)
XLA Ops:
  0.0 0.8 copy.11.aff_ref
  0.8 0.8 copy.12.ids_ref
  1.6 0.0 copy-start
  1.6 1.5 %copy-done = bf16[1,3584,256]{2,1,0:T(8,128)(2,1)S(1)} copy-done((bf16[1,3584,256]{2,1,0:T(8,128)(2,1)S(1)}, bf16[1,3584,256]{2,1,0:T(8,128)(2,1)}, u32[]{:S(2)}) %copy-start) | copy-done | bytes 1835032
  3.1 0.0 copy-start.1
  3.1 1.3 %copy-done.1 = bf16[160,3584]{1,0:T(8,128)(2,1)S(1)} copy-done((bf16[160,3584]{1,0:T(8,128)(2,1)S(1)}, bf16[160,3584]{1,0:T(8,128)(2,1)}, u32[]{:S(2)}) %copy-start.1) | copy-done | bytes 1146904
  4.4 0.0 copy-start.2
  4.4 1.2 %copy-done.2 = bf16[896,512]{1,0:T(8,128)(2,1)S(1)} copy-done((bf16[896,512]{1,0:T(8,128)(2,1)S(1)}, bf16[896,512]{1,0:T(8,128)(2,1)}, u32[]{:S(2)}) %copy-start.2) | copy-done | bytes 917528
  5.5 0.0 copy-start.3
  5.6 1.2 %copy-done.3 = bf16[896,512]{1,0:T(8,128)(2,1)S(1)} copy-done((bf16[896,512]{1,0:T(8,128)(2,1)S(1)}, bf16[896,512]{1,0:T(8,128)(2,1)}, u32[]{:S(2)}) %copy-start.3) | copy-done | bytes 917528
  6.7 0.0 copy-start.4
  6.7 1.2 %copy-done.4 = bf16[896,512]{1,0:T(8,128)(2,1)S(1)} copy-done((bf16[896,512]{1,0:T(8,128)(2,1)S(1)}, bf16[896,512]{1,0:T(8,128)(2,1)}, u32[]{:S(2)}) %copy-start.4) | copy-done | bytes 917528
  7.9 0.0 copy-start.5
  7.9 0.7 copy-done.5
  8.6 87.7 %shard_map.100 = bf16[160,896]{1,0:T(8,128)(2,1)S(1)} custom-call(bf16[160,3584]{1,0:T(8,128)(2,1)S(1)} %copy-done.1, f32[160,8]{1,0:T(8,128)S(1)} %copy.11.aff_ref, s32[160,8]{1,0:T(8,128)S(1)} %copy.12.ids_ref, s32[4]{0:T(128)S(1)} %copy-done.5, bf16[1,3584,256]{2,1,0:T(8,128)(2,1)S(1)} %copy-done, bf16[1,3584,256]{2,1,0:T(8,128)(2,1)} %ru_any.1, ...), custom_call_target="tpu_custom_call" | custom-call | tf_op jit(solution)/shard_map/pallas_call | solution.py:384
  96.3 0.7 copy.14
Async XLA Ops:
  1.6 1.5 %copy-start = (bf16[1,3584,256]{2,1,0:T(8,128)(2,1)S(1)}, bf16[1,3584,256]{2,1,0:T(8,128)(2,1)}, u32[]{:S(2)}) copy-start(bf16[1,3584,256]{2,1,0:T(8,128)(2,1)} %rg_any.1) | copy-start | bytes 5505028
  3.1 1.3 %copy-start.1 = (bf16[160,3584]{1,0:T(8,128)(2,1)S(1)}, bf16[160,3584]{1,0:T(8,128)(2,1)}, u32[]{:S(2)}) copy-start(bf16[160,3584]{1,0:T(8,128)(2,1)} %tok_any.1) | copy-start | bytes 3440644
  4.4 1.2 %copy-start.2 = (bf16[896,512]{1,0:T(8,128)(2,1)S(1)}, bf16[896,512]{1,0:T(8,128)(2,1)}, u32[]{:S(2)}) copy-start(bf16[896,512]{1,0:T(8,128)(2,1)} %sg_any.1) | copy-start | bytes 2752516
  5.5 1.2 %copy-start.3 = (bf16[896,512]{1,0:T(8,128)(2,1)S(1)}, bf16[896,512]{1,0:T(8,128)(2,1)}, u32[]{:S(2)}) copy-start(bf16[896,512]{1,0:T(8,128)(2,1)} %su_any.1) | copy-start | bytes 2752516
  6.7 1.2 %copy-start.4 = (bf16[896,512]{1,0:T(8,128)(2,1)S(1)}, bf16[896,512]{1,0:T(8,128)(2,1)}, u32[]{:S(2)}) copy-start(bf16[896,512]{1,0:T(8,128)(2,1)} %sd_any.1) | copy-start | bytes 2752516
  7.9 0.7 copy-start.5

commit v3 on v2

--- a/solution.py
+++ b/solution.py
@@ -81,6 +81,9 @@
     return mixed_out.astype(jnp.bfloat16)
 
 
+SEMAPHORES = 64
+VMEM_BYTES = 67043328
+RING = 4
 MESH = pl.DeviceIdType.MESH
 F32 = jnp.float32
 BF16 = jnp.bfloat16
@@ -101,10 +104,9 @@
     n_exp, n_ten,
     tok_any, aff_ref, ids_ref, cap_ref, rg_any, ru_any, rd_any, sg_any, su_any, sd_any,
     out_ref,
-    tok, wgu, wdn, rgw, ruw, rdw, xall, gown, gsend, gin, hall, weights,
+    tok, wgu, wdn, rgw, ruw, rdw, xall, xrel, gown, gpart, gsend, gin, hall, weights,
     rout, rin, ys, yin, yb, back, acc, osend, oin, rsend, rfin, routed,
-    lsem, ax_s, ax_r, af_s, af_r, bx_s, bx_r, bf_s, bf_r, c_s, c_r, h_s, h_r,
-    y_s, y_r, k_s, k_r, o_s, o_r, t_s, t_r,
+    lsem, ssem, rsem,
 ):
     e, t = lax.axis_index("expert"), lax.axis_index("tensor")
     core = lax.rem(t, 2)
@@ -115,15 +117,22 @@
     half_width = width // 2
     hidden = hall.shape[2]
     others = range(1, n_exp)
+    started = []
+
+    def link(src, dst, **device):
+        at = len(started)
+        copy = remote(src, dst, ssem.at[at], rsem.at[at], **device)
+        copy.start()
+        started.append(copy)
+        return copy
 
     def up(k):
-        return lax.rem(e + k, n_exp)
-
-    def down(k):
-        return lax.rem(e - k + n_exp, n_exp)
+        return lax.rem(e + k + n_exp, n_exp)
 
     def span(index, size, unit=128):
         return pl.ds(pl.multiple_of(index * size, unit), size)
+
+    right, left, opposite = up(1), up(-1), up(n_exp // 2)
 
     loads = [
         pltpu.make_async_copy(tok_any, tok, lsem.at[0]),
@@ -154,113 +163,140 @@
     pl.semaphore_wait(barrier, n_exp + n_ten - 2 + (e != t).astype(jnp.int32))
 
     mine = span(core, half, 16)
-    a_copy = {}
-    for k in others:
-        a_copy[k] = remote(
-            tok_any.at[mine, span(up(k), cols)], xall.at[e, mine, :],
-            ax_s.at[k - 1], ax_r.at[k - 1], expert=up(k),
-        )
-        a_copy[k].start()
+    large = (cols // 128 + 1) // 2 * 128
+    ahead, behind = up(1 - 2 * core), up(2 * core - 1)
+    x_copy = {}
+    for name, to in (("left", right), ("right", left)):
+        x_copy[name] = link(
+            tok_any.at[mine, span(to, cols)], xall.at[e, mine, :], expert=to
+        )
+    first = pl.multiple_of(opposite * cols, 128)
+    x_large = link(
+        tok_any.at[mine, pl.ds(first, large)], xrel.at[:, pl.ds(0, large)], expert=ahead
+    )
+    x_small = link(
+        tok_any.at[mine, pl.ds(first + large, cols - large)],
+        xrel.at[:, pl.ds(large, cols - large)],
+        expert=behind,
+    )
 
     lanes = n_exp * CAP
-    column = lax.broadcasted_iota(jnp.int32, (rows, lanes), 1)
-    expert_of, level = column // CAP, lax.rem(column, CAP)
+    line = lax.broadcasted_iota(jnp.int32, (lanes, rows), 0)
+    expert_of, level = line // CAP, lax.rem(line, CAP)
     ids, aff = ids_ref[...], aff_ref[...]
-    hit = jnp.zeros((rows, lanes), F32)
-    chosen = jnp.zeros((rows, lanes), F32)
-    for k in range(ids.shape[1]):
-        match = (ids[:, k : k + 1] == expert_of).astype(F32)
+    hit = jnp.zeros((lanes, rows), F32)
+    chosen = jnp.zeros((lanes, rows), F32)
+    for k in range(ids.shape[0]):
+        match = (ids[k : k + 1, :] == expert_of).astype(F32)
         hit += match
-        chosen += match * aff[:, k : k + 1]
-    share = 2.5 * chosen / jnp.sum(aff, axis=1, keepdims=True)
+        chosen += match * aff[k : k + 1, :]
+    share = 2.5 * chosen / jnp.sum(aff, axis=0, keepdims=True)
     earlier = (
-        lax.broadcasted_iota(jnp.int32, (rows, rows), 1)
-        < lax.broadcasted_iota(jnp.int32, (rows, rows), 0)
+        lax.broadcasted_iota(jnp.int32, (rows, rows), 0)
+        < lax.broadcasted_iota(jnp.int32, (rows, rows), 1)
     ).astype(BF16)
-    slot = jnp.dot(earlier, hit.astype(BF16), preferred_element_type=F32)
-    limit = jnp.zeros((rows, lanes), jnp.int32)
+    slot = jnp.dot(hit.astype(BF16), earlier, preferred_element_type=F32)
+    limit = jnp.zeros((lanes, rows), jnp.int32)
     for k in range(n_exp):
         limit = jnp.where(expert_of == k, cap_ref[k], limit)
     placed = (
         hit * (slot < limit.astype(F32)).astype(F32) * (slot == level.astype(F32)).astype(F32)
     )
-    weights[...] = placed * share
+    weights[...] = jnp.transpose(placed * share)
     loads[0].wait()
-    chosen_rows = jnp.dot(
-        jnp.transpose(placed).astype(BF16), tok[...], preferred_element_type=F32
-    ).astype(BF16).astype(F32)
+    chosen_rows = jnp.dot(placed.astype(BF16), tok[...], preferred_element_type=F32)
     for k in range(n_exp):
         rout[k] = chosen_rows[k * CAP : (k + 1) * CAP].astype(BF16)
+    rin[e] = rout[e]
+
+    x_pass = {}
+    for name, index in (("left", left), ("right", right)):
+        x_copy[name].wait_recv()
+        x_pass[name] = link(
+            xall.at[index, mine, :], xall.at[index, mine, :], tensor=partner
+        )
+    x_large.wait_recv()
+    whole_large = xall.at[behind, mine, pl.ds(0, large)]
+    x_large = link(xrel.at[:, pl.ds(0, large)], whole_large, expert=ahead)
+    x_small.wait_recv()
+    whole_small = xall.at[ahead, mine, pl.ds(large, cols - large)]
+    x_small = link(xrel.at[:, pl.ds(large, cols - large)], whole_small, expert=behind)
+    loads[1].wait()
+    loads[2].wait()
+
+    lower, upper = pl.ds(0, hidden), pl.ds(hidden, hidden)
+
+    def project(index):
+        return jnp.dot(xall[index], wgu[...], preferred_element_type=F32)
+
+    x_pass["left"].wait_recv()
+    found = project(left)
+    gsend[0] = found[:, :hidden].astype(BF16)
+    gpart[0] = found[:, hidden:]
+    g_left = link(gsend.at[0], gin.at[0], expert=left)
+    x_pass["right"].wait_recv()
+    found = project(right)
+    gsend[1] = found[:, hidden:].astype(BF16)
+    gpart[1] = found[:, :hidden]
+    g_right = link(gsend.at[1], gin.at[1], expert=right)
+
     side = span(core, half_width)
     b_copy = {}
     for k in others:
-        b_copy[k] = remote(
-            rout.at[up(k), :, side], rin.at[e, :, side],
-            bx_s.at[k - 1], bx_r.at[k - 1], expert=up(k),
-        )
-        b_copy[k].start()
-    rin[e] = rout[e]
-
-    order = [k for k in others if k != n_exp // 2] + [n_exp // 2]
-    af_copy, bf_copy = {}, {}
-    for k in order:
-        a_copy[k].wait_recv()
-        af_copy[k] = remote(
-            xall.at[down(k), mine, :], xall.at[down(k), mine, :],
-            af_s.at[k - 1], af_r.at[k - 1], tensor=partner,
-        )
-        af_copy[k].start()
-    loads[1].wait()
-    loads[2].wait()
-    c_copy = {}
-    for k in order:
-        af_copy[k].wait_recv()
-        gsend[k - 1] = jnp.dot(
-            xall[down(k)], wgu[...], preferred_element_type=F32
-        ).astype(BF16)
-        c_copy[k] = remote(
-            gsend.at[k - 1], gin.at[k - 1], c_s.at[k - 1], c_r.at[k - 1], expert=down(k)
-        )
-        c_copy[k].start()
-    for k in order:
+        b_copy[k] = link(rout.at[up(k), :, side], rin.at[e, :, side], expert=up(k))
+
+    x_large.wait_recv()
+    x_small.wait_recv()
+    x_far = link(
+        xall.at[opposite, mine, :], xall.at[opposite, mine, :], tensor=partner
+    )
+    x_far.wait_recv()
+    found = project(opposite)
+    gsend[2] = found[:, :hidden].astype(BF16)
+    g_low = link(gsend.at[2], gin.at[2], expert=right)
+    gsend[3] = found[:, hidden:].astype(BF16)
+    g_high = link(gsend.at[3], gin.at[3], expert=left)
+    gown[...] = jnp.dot(tok[:, span(e, cols)], wgu[...], preferred_element_type=F32)
+    b_pass = {}
+    for k in others:
         b_copy[k].wait_recv()
-        bf_copy[k] = remote(
-            rin.at[down(k), :, side], rin.at[down(k), :, side],
-            bf_s.at[k - 1], bf_r.at[k - 1], tensor=partner,
-        )
-        bf_copy[k].start()
-    gown[...] = jnp.dot(tok[:, span(e, cols)], wgu[...], preferred_element_type=F32)
+        b_pass[k] = link(
+            rin.at[up(-k), :, side], rin.at[up(-k), :, side], tensor=partner
+        )
+    g_low.wait_recv()
+    gsend[4] = (gpart[1] + gin[2].astype(F32)).astype(BF16)
+    g_low = link(gsend.at[4], gin.at[4], expert=right)
+    g_high.wait_recv()
+    gsend[5] = (gpart[0] + gin[3].astype(F32)).astype(BF16)
+    g_high = link(gsend.at[5], gin.at[5], expert=left)
 
     for load in loads[3:]:
         load.wait()
-    for k in order:
-        bf_copy[k].wait_recv()
+    for k in others:
+        b_pass[k].wait_recv()
     flat = jnp.concatenate([rin[k].astype(F32) for k in range(n_exp)], axis=0).astype(BF16)
     gate = jnp.dot(flat, rgw[...], preferred_element_type=F32)
-    upper = jnp.dot(flat, ruw[...], preferred_element_type=F32)
-    act = (gate * (1.0 / (1.0 + jnp.exp(-gate))) * upper).astype(BF16)
+    above = jnp.dot(flat, ruw[...], preferred_element_type=F32)
+    act = (gate * (1.0 / (1.0 + jnp.exp(-gate))) * above).astype(BF16)
     ys[...] = jnp.dot(act, rdw[...], preferred_element_type=F32).astype(BF16)
     y_copy = {}
     part = width // n_ten
     for k in range(1, n_ten):
         to = lax.rem(t + k, n_ten)
-        y_copy[k] = remote(
-            ys.at[:, span(to, part)], yin.at[k - 1], y_s.at[k - 1], y_r.at[k - 1], tensor=to
-        )
-        y_copy[k].start()
-
-    both = gown[...]
-    for k in order:
-        c_copy[k].wait_recv()
-        both = both + gin[k - 1].astype(F32)
-    gate = both[:, :hidden]
-    hall[e] = (gate * (1.0 / (1.0 + jnp.exp(-gate))) * both[:, hidden:]).astype(BF16)
-    h_copy = {}
-    for k in others:
-        h_copy[k] = remote(
-            hall.at[e], hall.at[e], h_s.at[k - 1], h_r.at[k - 1], expert=up(k)
-        )
-        h_copy[k].start()
+        y_copy[k] = link(ys.at[:, span(to, part)], yin.at[k - 1], tensor=to)
+
+    g_left.wait_recv()
+    g_right.wait_recv()
+    g_low.wait_recv()
+    g_high.wait_recv()
+    gate = gown[:, :hidden] + gin[0].astype(F32) + gin[4].astype(F32)
+    above = gown[:, hidden:] + gin[1].astype(F32) + gin[5].astype(F32)
+    hall[e] = (gate * (1.0 / (1.0 + jnp.exp(-gate))) * above).astype(BF16)
+    near, far = pl.ds(0, hidden // 2), pl.ds(hidden // 2, hidden // 2)
+    from_left = link(hall.at[e, :, near], hall.at[e, :, near], expert=right)
+    from_right = link(hall.at[e, :, far], hall.at[e, :, far], expert=left)
+    rest_left = link(hall.at[e, :, far], hall.at[e, :, far], expert=right)
+    rest_right = link(hall.at[e, :, near], hall.at[e, :, near], expert=left)
 
     total = ys[:, span(t, part)].astype(F32)
     for k in range(1, n_ten):
@@ -268,23 +304,30 @@
         total = total + yin[k - 1].astype(F32)
     for k in range(n_exp):
         yb[k] = total[k * CAP : (k + 1) * CAP].astype(BF16)
+    back[e] = yb[e]
+
+    from_left.wait_recv()
+    from_left = link(hall.at[left, :, near], hall.at[left, :, near], expert=right)
+    from_right.wait_recv()
+    from_right = link(hall.at[right, :, far], hall.at[right, :, far], expert=left)
     k_copy = {}
     for k in others:
-        k_copy[k] = remote(
-            yb.at[up(k)], back.at[e], k_s.at[k - 1], k_r.at[k - 1], expert=up(k)
-        )
-        k_copy[k].start()
-    back[e] = yb[e]
-
-    for k in order:
-        h_copy[k].wait_recv()
+        k_copy[k] = link(yb.at[up(k)], back.at[e], expert=up(k))
 
     def product(index):
         return lax.dot_general(
             hall[index], wdn[...], (((1,), (1,)), ((), ())), preferred_element_type=F32
         )
 
-    o_copy = []
+    acc[e] = product(e)
+    rest_left.wait_recv()
+    acc[left] = product(left)
+    rest_right.wait_recv()
+    acc[right] = product(right)
+    from_left.wait_recv()
+    from_right.wait_recv()
+    acc[opposite] = product(opposite)
+
     bits = n_ten.bit_length() - 1
     place = 0
     for s in range(bits):
@@ -295,24 +338,15 @@
         copies = []
         for i in range(count):
             sent = (2 * i + 1 - bit) * (1 << s) + low
-            osend[place + i] = (product(sent) if s == 0 else acc[sent]).astype(BF16)
-            copy = remote(
-                osend.at[place + i], oin.at[place + i],
-                o_s.at[place + i], o_r.at[place + i], tensor=peer,
-            )
-            copy.start()
-            copies.append(copy)
-        if s == 0:
-            for i in range(count):
-                kept = 2 * i + bit
-                acc[kept] = product(kept)
+            osend[place + i] = acc[sent].astype(BF16)
+            copies.append(link(osend.at[place + i], oin.at[place + i], tensor=peer))
         for i in range(count):
             kept = (2 * i + bit) * (1 << s) + low
             copies[i].wait_recv()
             acc[kept] = acc[kept] + oin[place + i].astype(F32)
-        o_copy += copies
         place += count
-    final = remote(rsend, rfin, t_s, t_r, expert=t, tensor=e)
+    at = len(started)
+    final = remote(rsend, rfin, ssem.at[at], rsem.at[at], expert=t, tensor=e)
 
     @pl.when(e != t)
     def _():
@@ -323,7 +357,7 @@
     def _():
         rfin[...] = acc[t].astype(BF16)
 
-    for k in order:
+    for k in others:
         k_copy[k].wait_recv()
     rows_back = jnp.concatenate([back[k].astype(F32) for k in range(n_exp)], axis=0)
     routed[...] = jnp.dot(
@@ -335,10 +369,7 @@
         final.wait()
 
     out_ref[...] = (rfin[...].astype(F32) + routed[...]).astype(BF16)
-    for group in (a_copy, af_copy, b_copy, bf_copy, c_copy, h_copy, y_copy, k_copy):
-        for copy in group.values():
-            copy.wait_send()
-    for copy in o_copy:
+    for copy in started:
         copy.wait_send()
 
 
@@ -357,9 +388,11 @@
         pltpu.VMEM(ru.shape[1:], BF16),
         pltpu.VMEM(rd.shape[1:], BF16),
         pltpu.VMEM((n_exp, rows, cols), BF16),
+        pltpu.VMEM((rows // 2, cols), BF16),
         pltpu.VMEM((rows, 2 * hidden), F32),
-        pltpu.VMEM((n_exp - 1, rows, 2 * hidden), BF16),
-        pltpu.VMEM((n_exp - 1, rows, 2 * hidden), BF16),
+        pltpu.VMEM((2, rows, hidden), F32),
+        pltpu.VMEM((6, rows, hidden), BF16),
+        pltpu.VMEM((6, rows, hidden), BF16),
         pltpu.VMEM((n_exp, rows, hidden), BF16),
         pltpu.VMEM((rows, n_exp * CAP), F32),
         pltpu.VMEM((n_exp, CAP, width), BF16),
@@ -375,12 +408,9 @@
         pltpu.VMEM((rows, part), BF16),
         pltpu.VMEM((rows, part), F32),
         pltpu.SemaphoreType.DMA((7,)),
+        pltpu.SemaphoreType.DMA((SEMAPHORES,)),
+        pltpu.SemaphoreType.DMA((SEMAPHORES,)),
     ]
-    scratch += [pltpu.SemaphoreType.DMA((n_exp - 1,))] * 12
-    scratch += [pltpu.SemaphoreType.DMA((n_ten - 1,))] * 2
-    scratch += [pltpu.SemaphoreType.DMA((n_exp - 1,))] * 2
-    scratch += [pltpu.SemaphoreType.DMA((n_ten - 1,))] * 2
-    scratch += [pltpu.SemaphoreType.DMA] * 2
     return pl.pallas_call(
         functools.partial(fused_kernel, n_exp, n_ten),
         out_shape=jax.ShapeDtypeStruct((rows, part), BF16),
@@ -388,23 +418,23 @@
         out_specs=vmem,
         scratch_shapes=scratch,
         compiler_params=pltpu.CompilerParams(
-            collective_id=0, has_side_effects=True, vmem_limit_bytes=48 * 1024 * 1024
+            collective_id=0, has_side_effects=True, vmem_limit_bytes=VMEM_BYTES
         ),
-    )(*args)
+    )(tokens, affinity.T, expert_ids.T, *args[3:])
 
 
 def fits(n_exp, n_ten, tokens, capacity, routed_gate, shared_gate):
     rows, width = tokens.shape
     return (
-        n_exp == n_ten
-        and n_ten >= 2
-        and n_ten & (n_ten - 1) == 0
+        n_exp == RING
+        and n_ten == n_exp
         and capacity.shape[0] == n_exp
         and routed_gate.shape[0] == 1
         and rows % 32 == 0
         and width % 256 == 0
+        and width // n_exp >= 256
         and width % (128 * n_exp) == 0
-        and shared_gate.shape[1] % 128 == 0
+        and shared_gate.shape[1] % 256 == 0
     )
 
 

time: 97.4 us -> 82.6 us (0.85)
  local copies, waits for them, and re-layouts: 9.25 us -> 1.69 us
  Pallas kernels: 87.7 us -> 80.7 us
    unnamed x15 -> x1, local copies, waits for them, and re-layouts: 9.25 us -> 1.69 us
    pallas_call x1, Pallas kernels: 87.7 us -> 80.7 us  [fused(): pl.pallas_call(functools.partial(fused_kernel, n_exp, n_ten), out_shape=j...]
where the time goes in v3:
time: 82.6 us; the launch traced here: 82.4 us
  Pallas kernels  80.7 us (98%)
  local copies, waits for them, and re-layouts  1.69 us (2%)
    pallas_call x1, Pallas kernels, fused(): pl.pallas_call(functools.partial(fused_kernel, n_exp, n_ten), out_shape=j...  80.7 us
    unnamed x1, local copies, waits for them, and re-layouts  1.69 us

profile of v3, /device:TPU:2, one launch (start us, length us, event | category | flops | bytes accessed | tf_op | source)
XLA Modules:
  0.0 82.4 jit_solution(4352460157987668518)
XLA Ops:
  0.0 80.7 %shard_map.100 = bf16[160,896]{1,0:T(8,128)(2,1)} custom-call(bf16[160,3584]{1,0:T(8,128)(2,1)} %tok_any.1, f32[8,160]{1,0:T(8,128)} %bitcast.2, s32[8,160]{1,0:T(8,128)} %bitcast.3, s32[4]{0:T(128)} %cap_ref.1, bf16[1,3584,256]{2,1,0:T(8,128)(2,1)} %rg_any.1, bf16[1,3584,256]{2,1,0:T(8,128)(2,1)} %ru_any.1, bf16[1,256,3584]{2,1,0:T(8,128)(2,1)} %rd_any.1, ...), custom_call_target="tpu_custom_call" | custom-call | tf_op jit(solution)/shard_map/pallas_call | solution.py:414
  80.7 1.7 %copy.12 = bf16[160,896]{1,0:T(8,128)(2,1)} copy(bf16[160,896]{1,0:T(8,128)(2,1)} %shard_map.100) | data formatting | bytes 573440

commit v4 on v3

--- a/solution.py
+++ b/solution.py
@@ -105,8 +105,8 @@
     tok_any, aff_ref, ids_ref, cap_ref, rg_any, ru_any, rd_any, sg_any, su_any, sd_any,
     out_ref,
     tok, wgu, wdn, rgw, ruw, rdw, xall, xrel, gown, gpart, gsend, gin, hall, weights,
-    rout, rin, ys, yin, yb, back, acc, osend, oin, rsend, rfin, routed,
-    lsem, ssem, rsem,
+    rout, rin, ys, yin, yb, back, acc, osend, oin, xsend, xin, fsend, rfin, routed,
+    lsem, ssem, rsem, cs, cr, xs, xr, fs, fr,
 ):
     e, t = lax.axis_index("expert"), lax.axis_index("tensor")
     core = lax.rem(t, 2)
@@ -143,24 +143,19 @@
         pltpu.make_async_copy(rd_any.at[0], rdw, lsem.at[5]),
         pltpu.make_async_copy(sd_any, wdn, lsem.at[6]),
     ]
-    for load in loads:
-        load.start()
+    loads[0].start()
 
     barrier = pltpu.get_barrier_semaphore()
-    for k in others:
-        pl.semaphore_signal(barrier, inc=1, device_id={"expert": up(k)}, device_id_type=MESH)
-    for k in range(1, n_ten):
-        pl.semaphore_signal(
-            barrier, inc=1, device_id={"tensor": lax.rem(t + k, n_ten)}, device_id_type=MESH
-        )
-
-    @pl.when(e != t)
-    def _():
-        pl.semaphore_signal(
-            barrier, inc=1, device_id={"expert": t, "tensor": e}, device_id_type=MESH
-        )
-
-    pl.semaphore_wait(barrier, n_exp + n_ten - 2 + (e != t).astype(jnp.int32))
+    for i in range(n_exp):
+        for j in range(n_ten):
+            if i or j:
+                pl.semaphore_signal(
+                    barrier,
+                    inc=1,
+                    device_id={"expert": up(i), "tensor": lax.rem(t + j, n_ten)},
+                    device_id_type=MESH,
+                )
+    pl.semaphore_wait(barrier, n_exp * n_ten - 1)
 
     mine = span(core, half, 16)
     large = (cols // 128 + 1) // 2 * 128
@@ -179,6 +174,9 @@
         xrel.at[:, pl.ds(large, cols - large)],
         expert=behind,
     )
+
+    for load in loads[1:]:
+        load.start()
 
     lanes = n_exp * CAP
     line = lax.broadcasted_iota(jnp.int32, (lanes, rows), 0)
@@ -319,43 +317,91 @@
             hall[index], wdn[...], (((1,), (1,)), ((), ())), preferred_element_type=F32
         )
 
-    acc[e] = product(e)
-    rest_left.wait_recv()
-    acc[left] = product(left)
-    rest_right.wait_recv()
-    acc[right] = product(right)
-    from_left.wait_recv()
-    from_right.wait_recv()
-    acc[opposite] = product(opposite)
-
-    bits = n_ten.bit_length() - 1
-    place = 0
-    for s in range(bits):
-        bit = lax.rem(t // (1 << s), 2)
-        low = lax.rem(t, 1 << s)
-        peer = t + (1 - 2 * bit) * (1 << s)
-        count = n_ten >> (s + 1)
-        copies = []
-        for i in range(count):
-            sent = (2 * i + 1 - bit) * (1 << s) + low
-            osend[place + i] = acc[sent].astype(BF16)
-            copies.append(link(osend.at[place + i], oin.at[place + i], tensor=peer))
-        for i in range(count):
-            kept = (2 * i + bit) * (1 << s) + low
-            copies[i].wait_recv()
-            acc[kept] = acc[kept] + oin[place + i].astype(F32)
-        place += count
-    at = len(started)
-    final = remote(rsend, rfin, ssem.at[at], rsem.at[at], expert=t, tensor=e)
-
-    @pl.when(e != t)
+    x_bit = t // 2
+    x_peer = lax.rem(t + 2, n_ten)
+    keep_half, give_half = span(x_bit, half, 16), span(1 - x_bit, half, 16)
+    blocks = [e, left, right, opposite]
+    arrivals = [[], [rest_left], [rest_right], [from_left, from_right]]
+
+    def core_copy(j):
+        return remote(osend.at[j], oin.at[j], cs.at[j], cr.at[j], tensor=partner)
+
+    def x_copy_of(j):
+        return remote(xsend.at[j], xin.at[j], xs.at[j], xr.at[j], tensor=x_peer)
+
+    def last_copy(j):
+        return remote(
+            fsend.at[j], rfin.at[keep_half, :], fs.at[j], fr.at[x_bit],
+            expert=blocks[j], tensor=e,
+        )
+
+    def compute(j):
+        for copy in arrivals[j]:
+            copy.wait_recv()
+        return product(blocks[j])
+
+    def give(j):
+        osend[j] = compute(j).astype(BF16)
+        core_copy(j).start()
+
+    def take(j):
+        acc[j] = compute(j)
+        core_copy(j).wait_recv()
+        xsend[j] = (acc[j, give_half, :] + oin[j, give_half, :].astype(F32)).astype(BF16)
+        x_copy_of(j).start()
+
+    def finish(j):
+        both = acc[j, keep_half, :] + oin[j, keep_half, :].astype(F32)
+        x_copy_of(j).wait_recv()
+        value = (both + xin[j].astype(F32)).astype(BF16)
+        if j:
+            fsend[j] = value
+            last_copy(j).start()
+        else:
+
+            @pl.when(e == t)
+            def _():
+                rfin[keep_half, :] = value
+
+            @pl.when(e != t)
+            def _():
+                fsend[j] = value
+                last_copy(j).start()
+
+    def settle(kept, given):
+        for j in given:
+            core_copy(j).wait_send()
+        for j in kept:
+            x_copy_of(j).wait_send()
+            if j:
+                last_copy(j).wait_send()
+            else:
+
+                @pl.when(e != t)
+                def _():
+                    last_copy(j).wait_send()
+
+    even = lax.rem(e + core, 2) == 0
+
+    @pl.when(even)
     def _():
-        rsend[...] = acc[t].astype(BF16)
-        final.start()
-
-    @pl.when(e == t)
+        take(0)
+        give(1)
+        give(2)
+        finish(0)
+        take(3)
+        finish(3)
+        settle((0, 3), (1, 2))
+
+    @pl.when(jnp.logical_not(even))
     def _():
-        rfin[...] = acc[t].astype(BF16)
+        give(0)
+        take(1)
+        take(2)
+        finish(1)
+        finish(2)
+        give(3)
+        settle((1, 2), (0, 3))
 
     for k in others:
         k_copy[k].wait_recv()
@@ -364,9 +410,14 @@
         weights[...], rows_back, preferred_element_type=F32, precision=lax.Precision.HIGHEST
     )
 
-    @pl.when(e != t)
-    def _():
-        final.wait()
+    for h in range(2):
+
+        @pl.when(jnp.logical_or(e != t, x_bit != h))
+        def _():
+            remote(
+                fsend.at[0], rfin.at[pl.ds(h * half, half), :], fs.at[0], fr.at[h],
+                expert=t, tensor=e,
+            ).wait_recv()
 
     out_ref[...] = (rfin[...].astype(F32) + routed[...]).astype(BF16)
     for copy in started:
@@ -401,16 +452,19 @@
         pltpu.VMEM((n_ten - 1, n_exp * CAP, part), BF16),
         pltpu.VMEM((n_exp, CAP, part), BF16),
         pltpu.VMEM((n_exp, CAP, part), BF16),
-        pltpu.VMEM((n_ten, rows, part), F32),
-        pltpu.VMEM((n_ten - 1, rows, part), BF16),
-        pltpu.VMEM((n_ten - 1, rows, part), BF16),
-        pltpu.VMEM((rows, part), BF16),
+        pltpu.VMEM((n_exp, rows, part), F32),
+        pltpu.VMEM((n_exp, rows, part), BF16),
+        pltpu.VMEM((n_exp, rows, part), BF16),
+        pltpu.VMEM((n_exp, rows // 2, part), BF16),
+        pltpu.VMEM((n_exp, rows // 2, part), BF16),
+        pltpu.VMEM((n_exp, rows // 2, part), BF16),
         pltpu.VMEM((rows, part), BF16),
         pltpu.VMEM((rows, part), F32),
         pltpu.SemaphoreType.DMA((7,)),
         pltpu.SemaphoreType.DMA((SEMAPHORES,)),
         pltpu.SemaphoreType.DMA((SEMAPHORES,)),
     ]
+    scratch += [pltpu.SemaphoreType.DMA((n_exp,))] * 5 + [pltpu.SemaphoreType.DMA((2,))]
     return pl.pallas_call(
         functools.partial(fused_kernel, n_exp, n_ten),
         out_shape=jax.ShapeDtypeStruct((rows, part), BF16),

time: 82.6 us -> 78.1 us (0.946)
  the two profiles are of different devices: /device:TPU:2 before, /device:TPU:11 now
where the time goes in v4:
time: 78.1 us; the launch traced here: 77.9 us
  Pallas kernels  76.2 us (98%)
  local copies, waits for them, and re-layouts  1.69 us (2%)
    pallas_call x1, Pallas kernels, fused(): pl.pallas_call(functools.partial(fused_kernel, n_exp, n_ten), out_shape=j...  76.2 us
    unnamed x1, local copies, waits for them, and re-layouts  1.69 us

profile of v4, /device:TPU:11, one launch (start us, length us, event | category | flops | bytes accessed | tf_op | source)
XLA Modules:
  0.0 77.9 jit_solution(3086711887094597306)
XLA Ops:
  0.0 76.2 %shard_map.100 = bf16[160,896]{1,0:T(8,128)(2,1)} custom-call(bf16[160,3584]{1,0:T(8,128)(2,1)} %tok_any.1, f32[8,160]{1,0:T(8,128)} %bitcast.2, s32[8,160]{1,0:T(8,128)} %bitcast.3, s32[4]{0:T(128)} %cap_ref.1, bf16[1,3584,256]{2,1,0:T(8,128)(2,1)} %rg_any.1, bf16[1,3584,256]{2,1,0:T(8,128)(2,1)} %ru_any.1, bf16[1,256,3584]{2,1,0:T(8,128)(2,1)} %rd_any.1, ...), custom_call_target="tpu_custom_call" | custom-call | tf_op jit(solution)/shard_map/pallas_call | solution.py:468
  76.2 1.7 %copy.12 = bf16[160,896]{1,0:T(8,128)(2,1)} copy(bf16[160,896]{1,0:T(8,128)(2,1)} %shard_map.100) | data formatting | bytes 573440

commit v5 on v4

--- a/solution.py
+++ b/solution.py
@@ -157,20 +157,21 @@
                 )
     pl.semaphore_wait(barrier, n_exp * n_ten - 1)
 
+    loads[0].wait()
     mine = span(core, half, 16)
     large = (cols // 128 + 1) // 2 * 128
     ahead, behind = up(1 - 2 * core), up(2 * core - 1)
     x_copy = {}
     for name, to in (("left", right), ("right", left)):
         x_copy[name] = link(
-            tok_any.at[mine, span(to, cols)], xall.at[e, mine, :], expert=to
+            tok.at[mine, span(to, cols)], xall.at[e, mine, :], expert=to
         )
     first = pl.multiple_of(opposite * cols, 128)
     x_large = link(
-        tok_any.at[mine, pl.ds(first, large)], xrel.at[:, pl.ds(0, large)], expert=ahead
+        tok.at[mine, pl.ds(first, large)], xrel.at[:, pl.ds(0, large)], expert=ahead
     )
     x_small = link(
-        tok_any.at[mine, pl.ds(first + large, cols - large)],
+        tok.at[mine, pl.ds(first + large, cols - large)],
         xrel.at[:, pl.ds(large, cols - large)],
         expert=behind,
     )
@@ -201,7 +202,6 @@
         hit * (slot < limit.astype(F32)).astype(F32) * (slot == level.astype(F32)).astype(F32)
     )
     weights[...] = jnp.transpose(placed * share)
-    loads[0].wait()
     chosen_rows = jnp.dot(placed.astype(BF16), tok[...], preferred_element_type=F32)
     for k in range(n_exp):
         rout[k] = chosen_rows[k * CAP : (k + 1) * CAP].astype(BF16)
@@ -268,21 +268,6 @@
     gsend[5] = (gpart[0] + gin[3].astype(F32)).astype(BF16)
     g_high = link(gsend.at[5], gin.at[5], expert=left)
 
-    for load in loads[3:]:
-        load.wait()
-    for k in others:
-        b_pass[k].wait_recv()
-    flat = jnp.concatenate([rin[k].astype(F32) for k in range(n_exp)], axis=0).astype(BF16)
-    gate = jnp.dot(flat, rgw[...], preferred_element_type=F32)
-    above = jnp.dot(flat, ruw[...], preferred_element_type=F32)
-    act = (gate * (1.0 / (1.0 + jnp.exp(-gate))) * above).astype(BF16)
-    ys[...] = jnp.dot(act, rdw[...], preferred_element_type=F32).astype(BF16)
-    y_copy = {}
-    part = width // n_ten
-    for k in range(1, n_ten):
-        to = lax.rem(t + k, n_ten)
-        y_copy[k] = link(ys.at[:, span(to, part)], yin.at[k - 1], tensor=to)
-
     g_left.wait_recv()
     g_right.wait_recv()
     g_low.wait_recv()
@@ -296,21 +281,42 @@
     rest_left = link(hall.at[e, :, far], hall.at[e, :, far], expert=right)
     rest_right = link(hall.at[e, :, near], hall.at[e, :, near], expert=left)
 
-    total = ys[:, span(t, part)].astype(F32)
-    for k in range(1, n_ten):
-        y_copy[k].wait_recv()
-        total = total + yin[k - 1].astype(F32)
-    for k in range(n_exp):
-        yb[k] = total[k * CAP : (k + 1) * CAP].astype(BF16)
-    back[e] = yb[e]
-
+    for load in loads[3:]:
+        load.wait()
+    for k in others:
+        b_pass[k].wait_recv()
+    flat = jnp.concatenate([rin[k].astype(F32) for k in range(n_exp)], axis=0).astype(BF16)
+    gate = jnp.dot(flat, rgw[...], preferred_element_type=F32)
+    above = jnp.dot(flat, ruw[...], preferred_element_type=F32)
+    act = (gate * (1.0 / (1.0 + jnp.exp(-gate))) * above).astype(BF16)
     from_left.wait_recv()
     from_left = link(hall.at[left, :, near], hall.at[left, :, near], expert=right)
     from_right.wait_recv()
     from_right = link(hall.at[right, :, far], hall.at[right, :, far], expert=left)
-    k_copy = {}
-    for k in others:
-        k_copy[k] = link(yb.at[up(k)], back.at[e], expert=up(k))
+    ys[...] = jnp.dot(act, rdw[...], preferred_element_type=F32).astype(BF16)
+    y_copy = {}
+    part = width // n_ten
+    for k in range(1, n_ten):
+        to = lax.rem(t + k, n_ten)
+        y_copy[k] = link(ys.at[:, span(to, part)], yin.at[k - 1], tensor=to)
+
+    k_at = len(started)
+
+    def k_copy(k):
+        return remote(
+            yb.at[up(k)], back.at[e], ssem.at[k_at + k - 1], rsem.at[k_at + k - 1], expert=up(k)
+        )
+
+    def join_routed():
+        total = ys[:, span(t, part)].astype(F32)
+        for k in range(1, n_ten):
+            y_copy[k].wait_recv()
+            total = total + yin[k - 1].astype(F32)
+        for k in range(n_exp):
+            yb[k] = total[k * CAP : (k + 1) * CAP].astype(BF16)
+        back[e] = yb[e]
+        for k in others:
+            k_copy(k).start()
 
     def product(index):
         return lax.dot_general(
@@ -389,6 +395,7 @@
         give(1)
         give(2)
         finish(0)
+        join_routed()
         take(3)
         finish(3)
         settle((0, 3), (1, 2))
@@ -401,10 +408,11 @@
         finish(1)
         finish(2)
         give(3)
+        join_routed()
         settle((1, 2), (0, 3))
 
     for k in others:
-        k_copy[k].wait_recv()
+        k_copy(k).wait()
     rows_back = jnp.concatenate([back[k].astype(F32) for k in range(n_exp)], axis=0)
     routed[...] = jnp.dot(
         weights[...], rows_back, preferred_element_type=F32, precision=lax.Precision.HIGHEST

time: 78.1 us -> 78 us (level)
  the two profiles are of different devices: /device:TPU:11 before, /device:TPU:15 now
where the time goes in v5:
time: 78 us; the launch traced here: 77.8 us
  Pallas kernels  76.1 us (98%)
  local copies, waits for them, and re-layouts  1.69 us (2%)
    pallas_call x1, Pallas kernels, fused(): pl.pallas_call(functools.partial(fused_kernel, n_exp, n_ten), out_shape=j...  76.1 us
    unnamed x1, local copies, waits for them, and re-layouts  1.69 us

profile of v5, /device:TPU:15, one launch (start us, length us, event | category | flops | bytes accessed | tf_op | source)
XLA Modules:
  0.0 77.8 jit_solution(6049906952552992495)
XLA Ops:
  0.0 76.1 %shard_map.100 = bf16[160,896]{1,0:T(8,128)(2,1)} custom-call(bf16[160,3584]{1,0:T(8,128)(2,1)} %tok_any.1, f32[8,160]{1,0:T(8,128)} %bitcast.2, s32[8,160]{1,0:T(8,128)} %bitcast.3, s32[4]{0:T(128)} %cap_ref.1, bf16[1,3584,256]{2,1,0:T(8,128)(2,1)} %rg_any.1, bf16[1,3584,256]{2,1,0:T(8,128)(2,1)} %ru_any.1, bf16[1,256,3584]{2,1,0:T(8,128)(2,1)} %rd_any.1, ...), custom_call_target="tpu_custom_call" | custom-call | tf_op jit(solution)/shard_map/pallas_call | solution.py:476
  76.1 1.7 %copy.12 = bf16[160,896]{1,0:T(8,128)(2,1)} copy(bf16[160,896]{1,0:T(8,128)(2,1)} %shard_map.100) | data formatting | bytes 573440
